TPU v7x, 32 devices: a whole 2x2x4 slice. The times are simulated.
32 devices in a mesh: day: 2 (over y), stu: 16 (over z, x, core).
Axes of the slice: x: 2, y: 2, z: 4, core: 2. Of those that a mesh axis runs over, the one named last changes fastest.
Arguments:
- performance: bfloat16 [64, 128, 1024], P('day', 'stu'), may hold values from -8 to 8
- student_factor: bfloat16 [128, 256], P('stu'), may hold values from -0.5 to 0.5
- skill_factor: bfloat16 [1024, 256], replicated, may hold values from -0.1875 to 0.1875
- day_prev: float32 [64, 256], P('day'), may hold values from -6 to 6
- ar_coef: float32 [7], replicated, may hold values from -0.3 to 0.3
Outputs:
- day_factor: float32 [64, 256], P('day', 'stu')
- residual: float32 [64, 256], P('day', 'stu')
All inputs are finite; a program needn't handle non-finite values.
Results may differ from a plain program's by a relative error of at most 0.0003.
Values sent between devices are 32-bit elements; how exact they have to be, the bound alone decides.
No kernel may reach another device: no remote copies, remote signals or barrier semaphores. Data moves between devices by JAX's collectives and lax.ppermute only.
A program may use at most 64 MiB of HBM per device.

v0:
```python
import jax
import jax.numpy as jnp
from jax import lax
from jax.sharding import PartitionSpec as P

LAGS = 7
ITERS = 3
smoothing = 1.0


def shifted(block, axis, distance):
    devices = range(lax.axis_size(axis))
    route = [(i - distance, i) for i in devices if i - distance in devices]
    return lax.ppermute(block, axis, route)


def filter_rows(extended, coef, count):
    out = extended[LAGS : LAGS + count]
    for lag in range(1, LAGS + 1):
        out = out - coef[lag - 1] * extended[LAGS - lag : LAGS - lag + count]
    return out


def smooth(values, coef):
    count = values.shape[0]
    below = shifted(values[count - LAGS :], "day", 1)
    ahead_core = filter_rows(jnp.concatenate([below, values], 0), coef, count)
    above = shifted(ahead_core[:LAGS], "day", -1)
    ahead = jnp.concatenate([ahead_core, above], 0)
    out = ahead[:count]
    for lag in range(1, LAGS + 1):
        out = out - coef[lag - 1] * ahead[lag : lag + count]
    return out


def with_gram(values, gram_part):
    return jnp.dot(
        lax.all_gather(values, "stu", axis=1, tiled=True),
        gram_part,
        precision=lax.Precision.HIGHEST,
        preferred_element_type=jnp.float32,
    )


def operate(values, gram_part, coef):
    return with_gram(values, gram_part) + smoothing * smooth(values, coef)


def global_total(value):
    return lax.psum(value, ("day", "stu"))


def summed_gram(local_gram):
    return lax.psum(local_gram, "stu")


def local(performance, student_factor, skill_factor, day_prev, ar_coef):
    days, students, skills = performance.shape
    rank = skill_factor.shape[1]
    proj = jnp.dot(
        performance.reshape(days * students, skills),
        skill_factor,
        preferred_element_type=jnp.float32,
    )
    proj = proj.reshape(days, students, rank)
    local_terms = jnp.sum(proj * student_factor.astype(jnp.float32)[None], axis=1)
    local_gram = jnp.dot(student_factor.T, student_factor, preferred_element_type=jnp.float32)
    skill_gram = jnp.dot(skill_factor.T, skill_factor, preferred_element_type=jnp.float32)
    columns = rank // lax.axis_size("stu")
    first_col = lax.axis_index("stu") * columns
    gram = summed_gram(local_gram) * skill_gram
    mttkrp = lax.psum_scatter(local_terms, "stu", scatter_dimension=1, tiled=True)
    gram_part = lax.dynamic_slice_in_dim(gram, first_col, columns, 1)
    day_factor = lax.dynamic_slice_in_dim(day_prev, first_col, columns, 1)
    residual = mttkrp - operate(day_factor, gram_part, ar_coef)
    direction = residual
    norm_now = global_total(jnp.sum(residual * residual))
    for step in range(ITERS):
        image = operate(direction, gram_part, ar_coef)
        alpha = norm_now / global_total(jnp.sum(direction * image))
        day_factor = day_factor + alpha * direction
        residual = residual - alpha * image
        norm_next = global_total(jnp.sum(residual * residual))
        direction = residual + norm_next / norm_now * direction
        norm_now = norm_next
    return (day_factor, residual)


def solution(mesh):
    return jax.shard_map(
        local,
        mesh=mesh,
        in_specs=(P("day", "stu", None), P("stu", None), P(), P("day", None), P()),
        out_specs=(P("day", "stu"), P("day", "stu")),
        check_vma=False,
    )
```

profile of v0, /device:TPU:14, one launch (start us, length us, event | category | flops | bytes accessed | tf_op | source)
XLA Modules:
  0.0 491.8 jit_solution(908321572501885240)
XLA Ops:
  9.6 1.7 fusion.139
  14.3 15.5 %all_gather.12 = f32[32,256]{0,1:T(8,128)S(1)} all-gather(f32[32,16]{0,1:T(8,128)S(1)} %copy.10), channel_id=1, replica_groups=mesh['day'=2,'stu'=16] {'stu'}, dimensions={1}, use_global_device_ids=true | all-gather | bytes 34816 | tf_op jit(solution)/shard_map/all_gather | solution.py:38
  29.8 4.5 fusion.120
  34.3 4.6 collective-permute-start.1
  38.9 64.2 %all-reduce.3.cloned.1.call-done = f32[256,256]{0,1:T(8,128)} async-done(((f32[256,256]{0,1:T(8,128)}), f32[256,256]{0,1:T(8,128)}) %all-reduce.3.cloned.1.call-update) | async-done | bytes 262160 | tf_op jit(solution)/shard_map/psum | solution.py:54
  103.8 57.7 %reduce-scatter.2.cloned.1.call-done = f32[32,16]{0,1:T(8,128)} async-done(((f32[32,256]{0,1:T(8,128)}), f32[32,16]{0,1:T(8,128)}) %reduce-scatter.2.cloned.1.call-update) | async-done | bytes 2064 | tf_op jit(solution)/shard_map/reduce_scatter | solution.py:72
  161.5 5.2 %fusion.104 = f32[32,16]{0,1:T(8,128)S(1)} fusion(f32[32,16]{0,1:T(8,128)} %reduce-scatter.2.cloned.1.call-done, f32[7,16]{0,1:T(8,128)S(1)} %collective-permute-done.1, f32[32,16]{0,1:T(8,128)S(1)} %fusion.120, f32[]{:T(128)} %bitcast.7, f32[]{:T(128)} %bitcast.6, f32[]{:T(128)} %bitcast.5, f32[]{:T(128)} %bitcast.4, f32[]{:T(128)} %bitcast.3, ...), kind=kOutput, calls=%fused_computation.173 | convolution fusion | flops 1584640 | bytes 55772 | tf_op jit(solution)/shard_map/dot_general | solution.py:37
  168.1 4.2 collective-permute-done.2
  172.3 4.5 fusion.86
  178.5 15.4 %all_gather.13 = f32[32,256]{0,1:T(8,128)S(1)} all-gather(f32[32,16]{0,1:T(8,128)S(1)} %fusion.104), channel_id=1, replica_groups=mesh['day'=2,'stu'=16] {'stu'}, dimensions={1}, use_global_device_ids=true | all-gather | bytes 34816 | tf_op jit(solution)/shard_map/all_gather | solution.py:38
  193.8 5.2 %multiply_reduce_fusion.4 = (f32[]{:T(128)}, f32[]{:T(128)}, f32[32,16]{0,1:T(8,128)S(1)}) fusion(f32[32,16]{0,1:T(8,128)S(1)} %fusion.104, f32[7,16]{0,1:T(8,128)S(1)} %collective-permute-done.3, f32[32,16]{0,1:T(8,128)S(1)} %fusion.86, f32[]{:T(128)} %bitcast.7, f32[]{:T(128)} %bitcast.6, f32[]{:T(128)} %bitcast.5, f32[]{:T(128)} %bitcast.4, ...), kind=kOutput, calls=%fused_computation.235 | convolution fusion | flops 1586174 | bytes 55780 | tf_op jit(solution)/shard_map/dot_general | solution.py:37
  199.0 44.1 %all-reduce = (f32[]{:T(128)}, f32[]{:T(128)}) all-reduce(f32[]{:T(128)} %get-tuple-element.3, f32[]{:T(128)} %get-tuple-element.2), channel_id=1, replica_groups=mesh['day'=2,'stu'=16] {'day','stu'}, use_global_device_ids=true, to_apply=%region_4.0 | all-reduce | flops 2 | bytes 16 | tf_op jit(solution)/shard_map/psum | solution.py:50
  245.1 38.6 %psum.52 = f32[]{:T(128)} all-reduce(f32[]{:T(128)} %multiply_reduce_fusion.3), channel_id=1, replica_groups=mesh['day'=2,'stu'=16] {'day','stu'}, use_global_device_ids=true, to_apply=%region_8.0 | all-reduce | flops 1 | bytes 8 | tf_op jit(solution)/shard_map/psum | solution.py:50
  286.4 4.2 collective-permute-done.4
  290.7 4.5 fusion.53
  296.8 18.0 %all_gather.14 = f32[32,256]{0,1:T(8,128)S(1)} all-gather(f32[32,16]{0,1:T(8,128)S(1)} %multiply_add_fusion.2), channel_id=1, replica_groups=mesh['day'=2,'stu'=16] {'stu'}, dimensions={1}, use_global_device_ids=true | all-gather | bytes 34816 | tf_op jit(solution)/shard_map/all_gather | solution.py:38
  314.8 5.2 %multiply_reduce_fusion.2 = (f32[]{:T(128)}, f32[32,16]{0,1:T(8,128)S(1)}) fusion(f32[32,16]{0,1:T(8,128)S(1)} %multiply_add_fusion.2, f32[7,16]{0,1:T(8,128)S(1)} %collective-permute-done.5, f32[32,16]{0,1:T(8,128)S(1)} %fusion.53, f32[]{:T(128)} %bitcast.7, f32[]{:T(128)} %bitcast.6, f32[]{:T(128)} %bitcast.5, f32[]{:T(128)} %bitcast.4, f32[]{:T(128)} %bitcast.3, ...), kind=kOutput, calls=%fused_computation.231 | convolution fusion | flops 1585151 | bytes 55776 | tf_op jit(solution)/shard_map/dot_general | solution.py:37
  320.0 43.0 %psum.53 = f32[]{:T(128)} all-reduce(f32[]{:T(128)} %get-tuple-element.10), channel_id=1, replica_groups=mesh['day'=2,'stu'=16] {'day','stu'}, use_global_device_ids=true, to_apply=%region_10.0 | all-reduce | flops 1 | bytes 8 | tf_op jit(solution)/shard_map/psum | solution.py:50
  364.8 39.0 %psum.54 = f32[]{:T(128)} all-reduce(f32[]{:T(128)} %get-tuple-element.8), channel_id=1, replica_groups=mesh['day'=2,'stu'=16] {'day','stu'}, use_global_device_ids=true, to_apply=%region_12.0 | all-reduce | flops 1 | bytes 8 | tf_op jit(solution)/shard_map/psum | solution.py:50
  406.5 4.2 collective-permute-done.6
  410.8 4.5 fusion.20
  416.9 17.6 %all_gather.15 = f32[32,256]{0,1:T(8,128)S(1)} all-gather(f32[32,16]{0,1:T(8,128)S(1)} %multiply_add_fusion.1), channel_id=1, replica_groups=mesh['day'=2,'stu'=16] {'stu'}, dimensions={1}, use_global_device_ids=true | all-gather | bytes 34816 | tf_op jit(solution)/shard_map/all_gather | solution.py:38
  434.5 5.1 %multiply_reduce_fusion = (f32[]{:T(128)}, f32[32,16]{0,1:T(8,128)S(1)}) fusion(f32[32,16]{0,1:T(8,128)S(1)} %multiply_add_fusion.1, f32[7,16]{0,1:T(8,128)S(1)} %collective-permute-done.7, f32[32,16]{0,1:T(8,128)S(1)} %fusion.20, f32[]{:T(128)} %bitcast.7, f32[]{:T(128)} %bitcast.6, f32[]{:T(128)} %bitcast.5, f32[]{:T(128)} %bitcast.4, f32[]{:T(128)} %bitcast.3, ...), kind=kOutput, calls=%fused_computation.227 | convolution fusion | flops 1585151 | bytes 55776 | tf_op jit(solution)/shard_map/dot_general | solution.py:37
  439.7 43.2 %psum.55 = f32[]{:T(128)} all-reduce(f32[]{:T(128)} %get-tuple-element.6), channel_id=1, replica_groups=mesh['day'=2,'stu'=16] {'day','stu'}, use_global_device_ids=true, to_apply=%region_14.0 | all-reduce | flops 1 | bytes 8 | tf_op jit(solution)/shard_map/psum | solution.py:50
  (41 shorter events, 17.0 us)
Async XLA Ops:
  7.2 4.8 copy-start
  7.2 4.8 copy-start.1
  7.2 95.9 %all-reduce.3.cloned.1.call-start = ((), (), s32[]{:S(2)}) async-start(), calls=%async_computation.2 | async-start | bytes 524288 | tf_op jit(solution)/shard_map/psum | solution.py:54
  8.3 21.6 %collective-permute-start = (f32[7,16]{0,1:T(8,128)S(1)}, f32[7,16]{0,1:T(8,128)S(1)}, u32[]{:S(2)}, u32[]{:S(2)}) collective-permute-start(f32[7,16]{0,1:T(8,128)S(1)} %slice.333), channel_id=1, source_target_pairs={{0,16},{1,17},{2,18},{3,19},{4,20},{5,21},{6,22},{7,23},{8,24},{9,... | collective-permute-start | bytes 1352 | tf_op jit(solution)/shard_map/ppermute | solution.py:14
  11.2 0.7 copy-start.2
  11.3 150.2 %reduce-scatter.2.cloned.1.call-start = ((), (), s32[]{:S(2)}) async-start(), calls=%async_computation.1 | async-start | bytes 139264 | tf_op jit(solution)/shard_map/reduce_scatter | solution.py:72
  13.0 0.7 copy-start.3
  34.3 69.5 %collective-permute-start.1 = (f32[7,16]{0,1:T(8,128)S(1)}, f32[7,16]{0,1:T(8,128)S(1)}, u32[]{:S(2)}, u32[]{:S(2)}) collective-permute-start(f32[7,16]{0,1:T(8,128)S(1)} %bitcast.27), channel_id=1, source_target_pairs={{16,0},{17,1},{18,2},{19,3},{20,4},{21,5},{22,6},{23,7},{24,8},{25... | collective-permute-start | bytes 1352 | tf_op jit(solution)/shard_map/ppermute | solution.py:14
  166.8 5.5 %collective-permute-start.2 = (f32[7,16]{0,1:T(8,128)S(1)}, f32[7,16]{0,1:T(8,128)S(1)}, u32[]{:S(2)}, u32[]{:S(2)}) collective-permute-start(f32[7,16]{0,1:T(8,128)S(1)} %slice.359), channel_id=1, source_target_pairs={{0,16},{1,17},{2,18},{3,19},{4,20},{5,21},{6,22},{7,23},{8,24},{9,... | collective-permute-start | bytes 1352 | tf_op jit(solution)/shard_map/ppermute | solution.py:14
  176.8 17.0 %collective-permute-start.3 = (f32[7,16]{0,1:T(8,128)S(1)}, f32[7,16]{0,1:T(8,128)S(1)}, u32[]{:S(2)}, u32[]{:S(2)}) collective-permute-start(f32[7,16]{0,1:T(8,128)S(1)} %bitcast.29), channel_id=1, source_target_pairs={{16,0},{17,1},{18,2},{19,3},{20,4},{21,5},{22,6},{23,7},{24,8},{25... | collective-permute-start | bytes 1352 | tf_op jit(solution)/shard_map/ppermute | solution.py:14
  285.1 5.5 %collective-permute-start.4 = (f32[7,16]{0,1:T(8,128)S(1)}, f32[7,16]{0,1:T(8,128)S(1)}, u32[]{:S(2)}, u32[]{:S(2)}) collective-permute-start(f32[7,16]{0,1:T(8,128)S(1)} %slice.385), channel_id=1, source_target_pairs={{0,16},{1,17},{2,18},{3,19},{4,20},{5,21},{6,22},{7,23},{8,24},{9,... | collective-permute-start | bytes 1352 | tf_op jit(solution)/shard_map/ppermute | solution.py:14
  295.1 19.6 %collective-permute-start.5 = (f32[7,16]{0,1:T(8,128)S(1)}, f32[7,16]{0,1:T(8,128)S(1)}, u32[]{:S(2)}, u32[]{:S(2)}) collective-permute-start(f32[7,16]{0,1:T(8,128)S(1)} %bitcast.30), channel_id=1, source_target_pairs={{16,0},{17,1},{18,2},{19,3},{20,4},{21,5},{22,6},{23,7},{24,8},{25... | collective-permute-start | bytes 1352 | tf_op jit(solution)/shard_map/ppermute | solution.py:14
  405.3 5.5 %collective-permute-start.6 = (f32[7,16]{0,1:T(8,128)S(1)}, f32[7,16]{0,1:T(8,128)S(1)}, u32[]{:S(2)}, u32[]{:S(2)}) collective-permute-start(f32[7,16]{0,1:T(8,128)S(1)} %slice.411), channel_id=1, source_target_pairs={{0,16},{1,17},{2,18},{3,19},{4,20},{5,21},{6,22},{7,23},{8,24},{9,... | collective-permute-start | bytes 1352 | tf_op jit(solution)/shard_map/ppermute | solution.py:14
  415.3 19.3 %collective-permute-start.7 = (f32[7,16]{0,1:T(8,128)S(1)}, f32[7,16]{0,1:T(8,128)S(1)}, u32[]{:S(2)}, u32[]{:S(2)}) collective-permute-start(f32[7,16]{0,1:T(8,128)S(1)} %bitcast.28), channel_id=1, source_target_pairs={{16,0},{17,1},{18,2},{19,3},{20,4},{21,5},{22,6},{23,7},{24,8},{25... | collective-permute-start | bytes 1352 | tf_op jit(solution)/shard_map/ppermute | solution.py:14
Sparse Core Ops, SparseCore 0:
  11.4 91.6 all-reduce.2
  106.5 54.8 reduce-scatter.1
where the time goes:
time: 494 us; the launch traced here: 492 us
  blocking collectives  274 us (55%)
  waiting for transfers between devices  135 us (27%)
  matrix products  23.1 us (5%)
  between operations  20.9 us (4%)
  other arithmetic  20.4 us (4%)
  starting transfers between devices  14.7 us (3%)
    psum x5, blocking collectives, global_total(): return lax.psum(value, ('day', 'stu'))  208 us
    all_gather x4, blocking collectives, with_gram(): lax.all_gather(values, 'stu', axis=1, tiled=True)  66.5 us
    psum x1, waiting for transfers between devices, summed_gram(): return lax.psum(local_gram, 'stu')  64.2 us
    reduce_scatter x1, waiting for transfers between devices, local(): lax.psum_scatter(local_terms, 'stu', scatter_dimension=1, tiled=True)  57.7 us
    dot_general x4, matrix products, with_gram(): jnp.dot(lax.all_gather(values, 'stu', axis=1, tiled=True), gram_part, pre...  20.8 us
    sub x4, other arithmetic, filter_rows(): out = out - coef[lag - 1] * extended[LAGS - lag:LAGS - lag + count]  17.8 us
    ppermute x8, starting transfers between devices, shifted(): return lax.ppermute(block, axis, route)  14.6 us
    ppermute x8, waiting for transfers between devices, shifted(): return lax.ppermute(block, axis, route)  12.7 us
  transfers between devices with their start and end apart: 10, of which 5 were waited for; matrix products, arithmetic and copies ran while one was open for 2% of the time, Pallas kernels for 0%

commit v1 on v0

--- a/solution.py
+++ b/solution.py
@@ -6,6 +6,19 @@
 LAGS = 7
 ITERS = 3
 smoothing = 1.0
+
+
+def gather_around(shard, axis, dim):
+    ways = lax.axis_size(axis)
+    up = [(d, (d + 1) % ways) for d in range(ways)]
+    down = [(d, (d - 1) % ways) for d in range(ways)]
+    earlier, later = ([shard], [shard])
+    for _ in range(ways // 2):
+        earlier.append(lax.ppermute(earlier[-1], axis, up))
+    for _ in range((ways - 1) // 2):
+        later.append(lax.ppermute(later[-1], axis, down))
+    line = jnp.concatenate([*earlier[::-1], *later[1:]], axis=dim)
+    return jnp.roll(line, (lax.axis_index(axis) - ways // 2) * shard.shape[dim], axis=dim)
 
 
 def shifted(block, axis, distance):
@@ -35,7 +48,7 @@
 
 def with_gram(values, gram_part):
     return jnp.dot(
-        lax.all_gather(values, "stu", axis=1, tiled=True),
+        gather_around(values, "stu", 1),
         gram_part,
         precision=lax.Precision.HIGHEST,
         preferred_element_type=jnp.float32,

time: 494 us -> 572 us (1.16)
  starting transfers between devices: 14.7 us -> 94.2 us
  blocking collectives: 274 us -> 245 us
  waiting for transfers between devices: 135 us -> 157 us
    ppermute x0 -> x60, starting transfers between devices: none -> 74.7 us  [the longest x32 48.2 us: gather_around(): earlier.append(lax.ppermute(earlier[-1], axis, up))]
    all_gather x4 -> x0, blocking collectives: 66.5 us -> none  [with_gram(): lax.all_gather(values, 'stu', axis=1, tiled=True)]
    psum x5, blocking collectives: 208 us -> 245 us  [global_total(): return lax.psum(value, ('day', 'stu'))]
    ppermute x0 -> x60, waiting for transfers between devices: none -> 23.5 us  [the longest x32 22.9 us: gather_around(): earlier.append(lax.ppermute(earlier[-1], axis, up))]
    ppermute x8, waiting for transfers between devices: 12.7 us -> 2.95 us  [shifted(): return lax.ppermute(block, axis, route)]
    psum x1, waiting for transfers between devices: 64.2 us -> 72.8 us  [summed_gram(): return lax.psum(local_gram, 'stu')]
  transfers between devices with their start and end apart: 10 -> 70, of which waited for: 5 -> 31; matrix products, arithmetic and copies ran while one was open for 2% -> 5% of each run, Pallas kernels for 0% -> 0%
where the time goes in v1:
time: 572 us; the launch traced here: 569 us
  blocking collectives  245 us (43%)
  waiting for transfers between devices  157 us (27%)
  starting transfers between devices  94.2 us (16%)
  matrix products  22.8 us (4%)
  between operations  21 us (4%)
  other arithmetic  20.6 us (4%)
  local copies, waits for them, and re-layouts  7.91 us (1%)
    psum x5, blocking collectives, global_total(): return lax.psum(value, ('day', 'stu'))  245 us
    psum x1, waiting for transfers between devices, summed_gram(): return lax.psum(local_gram, 'stu')  72.8 us
    reduce_scatter x1, waiting for transfers between devices, local(): lax.psum_scatter(local_terms, 'stu', scatter_dimension=1, tiled=True)  57.7 us
    ppermute x32, starting transfers between devices, gather_around(): earlier.append(lax.ppermute(earlier[-1], axis, up))  48.2 us
    ppermute x28, starting transfers between devices, gather_around(): later.append(lax.ppermute(later[-1], axis, down))  26.5 us
    ppermute x32, waiting for transfers between devices, gather_around(): earlier.append(lax.ppermute(earlier[-1], axis, up))  22.9 us
    dot_general x4, matrix products, with_gram(): jnp.dot(gather_around(values, 'stu', 1), gram_part, precision=lax.Precisi...  21.2 us
    ppermute x8, starting transfers between devices, shifted(): return lax.ppermute(block, axis, route)  19.5 us
  transfers between devices with their start and end apart: 70, of which 31 were waited for; matrix products, arithmetic and copies ran while one was open for 5% of the time, Pallas kernels for 0%

profile of v1, /device:TPU:14, one launch (start us, length us, event | category | flops | bytes accessed | tf_op | source)
XLA Modules:
  0.0 568.8 jit_solution(1478813211921856361)
XLA Ops:
  28.1 3.1 collective-permute-start.6
  32.1 3.1 collective-permute-start.7
  35.2 4.5 fusion.142
  39.7 4.3 collective-permute-start.16
  45.3 72.8 %all-reduce.3.cloned.1.call-done = f32[256,256]{0,1:T(8,128)} async-done(((f32[256,256]{0,1:T(8,128)}), f32[256,256]{0,1:T(8,128)}) %all-reduce.3.cloned.1.call-update) | async-done | bytes 262160 | tf_op jit(solution)/shard_map/psum | solution.py:67
  118.8 57.7 %reduce-scatter.2.cloned.1.call-done = f32[32,16]{0,1:T(8,128)} async-done(((f32[32,256]{0,1:T(8,128)}), f32[32,16]{0,1:T(8,128)}) %reduce-scatter.2.cloned.1.call-update) | async-done | bytes 2064 | tf_op jit(solution)/shard_map/reduce_scatter | solution.py:85
  176.5 5.3 fusion.26
  204.9 3.2 collective-permute-start.24
  209.0 4.5 fusion.110
  213.5 3.4 collective-permute-start.33
  218.2 5.3 multiply_reduce_fusion.4
  223.6 54.8 %all-reduce = (f32[]{:T(128)}, f32[]{:T(128)}) all-reduce(f32[]{:T(128)} %get-tuple-element.4, f32[]{:T(128)} %get-tuple-element.3), channel_id=1, replica_groups=mesh['day'=2,'stu'=16] {'day','stu'}, use_global_device_ids=true, to_apply=%region_4.6 | all-reduce | flops 2 | bytes 16 | tf_op jit(solution)/shard_map/psum | solution.py:63
  280.3 39.8 %psum.52 = f32[]{:T(128)} all-reduce(f32[]{:T(128)} %multiply_reduce_fusion.3), channel_id=1, replica_groups=mesh['day'=2,'stu'=16] {'day','stu'}, use_global_device_ids=true, to_apply=%region_8.10 | all-reduce | flops 1 | bytes 8 | tf_op jit(solution)/shard_map/psum | solution.py:63
  345.1 3.2 collective-permute-start.41
  349.3 4.5 fusion.78
  353.8 3.4 collective-permute-start.50
  358.5 5.3 multiply_reduce_fusion.2
  363.8 55.5 %psum.53 = f32[]{:T(128)} all-reduce(f32[]{:T(128)} %get-tuple-element.17), channel_id=1, replica_groups=mesh['day'=2,'stu'=16] {'day','stu'}, use_global_device_ids=true, to_apply=%region_10.12 | all-reduce | flops 1 | bytes 8 | tf_op jit(solution)/shard_map/psum | solution.py:63
  421.2 39.8 %psum.54 = f32[]{:T(128)} all-reduce(f32[]{:T(128)} %get-tuple-element.7), channel_id=1, replica_groups=mesh['day'=2,'stu'=16] {'day','stu'}, use_global_device_ids=true, to_apply=%region_12.14 | all-reduce | flops 1 | bytes 8 | tf_op jit(solution)/shard_map/psum | solution.py:63
  486.0 3.2 collective-permute-start.58
  490.2 4.5 fusion.46
  494.7 3.4 collective-permute-start.67
  499.4 5.3 multiply_reduce_fusion
  504.6 55.4 %psum.55 = f32[]{:T(128)} all-reduce(f32[]{:T(128)} %get-tuple-element.19), channel_id=1, replica_groups=mesh['day'=2,'stu'=16] {'day','stu'}, use_global_device_ids=true, to_apply=%region_14.16 | all-reduce | flops 1 | bytes 8 | tf_op jit(solution)/shard_map/psum | solution.py:63
  (224 shorter events, 102.5 us)
Async XLA Ops:
  7.2 110.9 %all-reduce.3.cloned.1.call-start = ((), (), s32[]{:S(2)}) async-start(), calls=%async_computation.2 | async-start | bytes 524288 | tf_op jit(solution)/shard_map/psum | solution.py:67
  11.3 4.7 collective-permute-start.9
  14.7 20.5 %collective-permute-start.15 = (f32[7,16]{0,1:T(8,128)S(1)}, f32[7,16]{0,1:T(8,128)S(1)}, u32[]{:S(2)}, u32[]{:S(2)}) collective-permute-start(f32[7,16]{0,1:T(8,128)S(1)} %slice.333), channel_id=1, source_target_pairs={{0,16},{1,17},{2,18},{3,19},{4,20},{5,21},{6,22},{7,23},{8,24},{9,... | collective-permute-start | bytes 1352 | tf_op jit(solution)/shard_map/ppermute | solution.py:27
  20.3 156.2 %reduce-scatter.2.cloned.1.call-start = ((), (), s32[]{:S(2)}) async-start(), calls=%async_computation.1 | async-start | bytes 139264 | tf_op jit(solution)/shard_map/reduce_scatter | solution.py:85
  31.9 13.1 %collective-permute-start.14 = (f32[32,16]{0,1:T(8,128)S(1)}, f32[32,16]{0,1:T(8,128)S(1)}, u32[]{:S(2)}, u32[]{:S(2)}) collective-permute-start(f32[32,16]{0,1:T(8,128)S(1)} %collective-permute-done.13), channel_id=1, source_target_pairs={{0,15},{1,0},{2,1},{3,2},{4,3},{5,4},{6,5},{7,6},{8,7},{9,8},{10,9... | collective-permute-start | bytes 6152 | tf_op jit(solution)/shard_map/ppermute | solution.py:19
  32.1 13.0 %collective-permute-start.7 = (f32[32,16]{0,1:T(8,128)S(1)}, f32[32,16]{0,1:T(8,128)S(1)}, u32[]{:S(2)}, u32[]{:S(2)}) collective-permute-start(f32[32,16]{0,1:T(8,128)S(1)} %collective-permute-done.6), channel_id=1, source_target_pairs={{0,1},{1,2},{2,3},{3,4},{4,5},{5,6},{6,7},{7,8},{8,9},{9,10},{10,1... | collective-permute-start | bytes 6152 | tf_op jit(solution)/shard_map/ppermute | solution.py:17
  39.7 79.1 %collective-permute-start.16 = (f32[7,16]{0,1:T(8,128)S(1)}, f32[7,16]{0,1:T(8,128)S(1)}, u32[]{:S(2)}, u32[]{:S(2)}) collective-permute-start(f32[7,16]{0,1:T(8,128)S(1)} %bitcast.23), channel_id=1, source_target_pairs={{16,0},{17,1},{18,2},{19,3},{20,4},{21,5},{22,6},{23,7},{24,8},{25... | collective-permute-start | bytes 1352 | tf_op jit(solution)/shard_map/ppermute | solution.py:27
  199.4 5.4 collective-permute-start.30
  203.5 5.5 collective-permute-start.32
  204.9 13.0 %collective-permute-start.31 = (f32[32,16]{0,1:T(8,128)S(1)}, f32[32,16]{0,1:T(8,128)S(1)}, u32[]{:S(2)}, u32[]{:S(2)}) collective-permute-start(f32[32,16]{0,1:T(8,128)S(1)} %collective-permute-done.30), channel_id=1, source_target_pairs={{0,15},{1,0},{2,1},{3,2},{4,3},{5,4},{6,5},{7,6},{8,7},{9,8},{10,9... | collective-permute-start | bytes 6152 | tf_op jit(solution)/shard_map/ppermute | solution.py:19
  204.9 13.1 %collective-permute-start.24 = (f32[32,16]{0,1:T(8,128)S(1)}, f32[32,16]{0,1:T(8,128)S(1)}, u32[]{:S(2)}, u32[]{:S(2)}) collective-permute-start(f32[32,16]{0,1:T(8,128)S(1)} %collective-permute-done.23), channel_id=1, source_target_pairs={{0,1},{1,2},{2,3},{3,4},{4,5},{5,6},{6,7},{7,8},{8,9},{9,10},{10,1... | collective-permute-start | bytes 6152 | tf_op jit(solution)/shard_map/ppermute | solution.py:17
  213.5 4.7 collective-permute-start.33
  339.7 5.4 collective-permute-start.47
  340.5 4.6 collective-permute-start.40
  343.8 5.5 collective-permute-start.49
  345.1 13.0 %collective-permute-start.48 = (f32[32,16]{0,1:T(8,128)S(1)}, f32[32,16]{0,1:T(8,128)S(1)}, u32[]{:S(2)}, u32[]{:S(2)}) collective-permute-start(f32[32,16]{0,1:T(8,128)S(1)} %collective-permute-done.47), channel_id=1, source_target_pairs={{0,15},{1,0},{2,1},{3,2},{4,3},{5,4},{6,5},{7,6},{8,7},{9,8},{10,9... | collective-permute-start | bytes 6152 | tf_op jit(solution)/shard_map/ppermute | solution.py:19
  345.1 13.1 %collective-permute-start.41 = (f32[32,16]{0,1:T(8,128)S(1)}, f32[32,16]{0,1:T(8,128)S(1)}, u32[]{:S(2)}, u32[]{:S(2)}) collective-permute-start(f32[32,16]{0,1:T(8,128)S(1)} %collective-permute-done.40), channel_id=1, source_target_pairs={{0,1},{1,2},{2,3},{3,4},{4,5},{5,6},{6,7},{7,8},{8,9},{9,10},{10,1... | collective-permute-start | bytes 6152 | tf_op jit(solution)/shard_map/ppermute | solution.py:17
  353.8 4.7 collective-permute-start.50
  480.6 5.4 collective-permute-start.64
  481.4 4.6 collective-permute-start.57
  484.6 5.5 collective-permute-start.66
  486.0 13.0 %collective-permute-start.65 = (f32[32,16]{0,1:T(8,128)S(1)}, f32[32,16]{0,1:T(8,128)S(1)}, u32[]{:S(2)}, u32[]{:S(2)}) collective-permute-start(f32[32,16]{0,1:T(8,128)S(1)} %collective-permute-done.64), channel_id=1, source_target_pairs={{0,15},{1,0},{2,1},{3,2},{4,3},{5,4},{6,5},{7,6},{8,7},{9,8},{10,9... | collective-permute-start | bytes 6152 | tf_op jit(solution)/shard_map/ppermute | solution.py:19
  486.0 13.1 %collective-permute-start.58 = (f32[32,16]{0,1:T(8,128)S(1)}, f32[32,16]{0,1:T(8,128)S(1)}, u32[]{:S(2)}, u32[]{:S(2)}) collective-permute-start(f32[32,16]{0,1:T(8,128)S(1)} %collective-permute-done.57), channel_id=1, source_target_pairs={{0,1},{1,2},{2,3},{3,4},{4,5},{5,6},{6,7},{7,8},{8,9},{9,10},{10,1... | collective-permute-start | bytes 6152 | tf_op jit(solution)/shard_map/ppermute | solution.py:17
  494.7 4.7 collective-permute-start.67
  (50 other events, 206.3 us)
Sparse Core Ops, SparseCore 0:
  20.5 97.5 all-reduce.2
  121.6 54.9 reduce-scatter.1
